TPU v7x, 256 devices: a whole 4x4x8 slice. The times are simulated.
256 devices in a mesh: dp: 32 (over x, z), expert: 8 (over y, core).
Axes of the slice: x: 4, y: 4, z: 8, core: 2. Of those that a mesh axis runs over, the one named last changes fastest.
Arguments:
- text_embed: bfloat16 [16384, 2048], P(('dp', 'expert')), may hold values from -6 to 6
- image_feats: bfloat16 [8192, 4608], P(('dp', 'expert')), may hold values from -6 to 6
- tile_pos: int32 [8192], P(('dp', 'expert')), may hold values from 0 to 16383, as said below
- proj_in: bfloat16 [4608, 2048], P(None, 'expert'), may hold values from -0.09375 to 0.09375
- proj_out: bfloat16 [2048, 2048], P('expert'), may hold values from -0.125 to 0.125
- norm_gain: float32 [2048], replicated, may hold values from 0.1 to 1.9
- shared_gate: bfloat16 [2048, 2816], P(None, 'expert'), may hold values from -0.125 to 0.125
- shared_up: bfloat16 [2048, 2816], P(None, 'expert'), may hold values from -0.125 to 0.125
- shared_down: bfloat16 [2816, 2048], P('expert'), may hold values from -0.109375 to 0.109375
- expert_gate: bfloat16 [32, 2048, 1408], P('dp', None, 'expert'), may hold values from -0.125 to 0.125
- expert_up: bfloat16 [32, 2048, 1408], P('dp', None, 'expert'), may hold values from -0.125 to 0.125
- expert_down: bfloat16 [32, 1408, 2048], P('dp', 'expert'), may hold values from -0.15625 to 0.15625
- route_ids: int32 [16384, 2], P(('dp', 'expert')), may hold values from 0 to 31, all different within a row; in each aligned block of 512 rows (0 to 511, 512 to 1023, ...) at most 48 rows name the same one
- route_wts: int32 [16384, 2], P(('dp', 'expert')), may hold values from 1 to 65535
Outputs:
- block_out: bfloat16 [16384, 2048], P(('dp', 'expert'))
Inputs may be any that keep to these rules, and one draw needn't show every extreme that they name: `tile_pos`: positions are distinct. The 32 image tokens of one device go 1 to each index of dp, always to rows held by the devices with the sender's own index of expert. `route_ids`: in each aligned block of 512 rows no expert is named by more than 48 rows, a bound that some block reaches.
All inputs are finite; a program needn't handle non-finite values.
Results may differ from a plain program's by a relative error of at most 0.018.
Values may be sent and summed in bfloat16 or wider, within the bound.
A program may use at most 128 MiB of HBM per device.

v0:
```python
import jax
import jax.numpy as jnp
from jax import lax
from jax.sharding import PartitionSpec as P


def normalize(rows, norm_gain):
    rows_f = rows.astype(jnp.float32)
    meansq = jnp.mean(rows_f * rows_f, axis=-1, keepdims=True) + 1e-06
    return (rows_f * lax.rsqrt(meansq) * norm_gain).astype(jnp.bfloat16)


def select_dot(sel, rows):
    return jnp.dot(sel, rows, preferred_element_type=jnp.float32)


def shards(
    text_embed,
    image_feats,
    tile_pos,
    proj_in,
    proj_out,
    norm_gain,
    shared_gate,
    shared_up,
    shared_down,
    expert_gate,
    expert_up,
    expert_down,
    route_ids,
    route_wts,
):
    bf16, f32 = (jnp.bfloat16, jnp.float32)
    tok_dev, width_model = text_embed.shape
    img_dev, width_vis = image_feats.shape
    n_data = lax.axis_size("dp")
    n_group = lax.axis_size("expert")
    peer = img_dev // n_data
    my_place = lax.axis_index("expert")
    dest_index = tile_pos // tok_dev // n_group
    order = jnp.argsort(dest_index, stable=True)
    offs_sorted = (tile_pos[order] % tok_dev).astype(bf16)
    pad = 128
    packed = jnp.concatenate(
        [image_feats[order], jnp.broadcast_to(offs_sorted[:, None], (img_dev, pad))], axis=1
    ).reshape(n_data, peer, width_vis + pad)
    moved = lax.all_to_all(packed, "dp", split_axis=0, concat_axis=0, tiled=True)
    moved = moved.reshape(img_dev, width_vis + pad)
    moved_feats = moved[:, :width_vis]
    moved_offs = moved[:, width_vis].astype(jnp.int32)
    feats = lax.all_gather(moved_feats, "expert", axis=0, tiled=True)
    vis_hidden = jax.nn.gelu(
        jnp.dot(feats, proj_in, preferred_element_type=f32), approximate=True
    ).astype(bf16)
    partial_proj = jnp.dot(vis_hidden, proj_out, preferred_element_type=f32).astype(bf16)
    projected = lax.psum_scatter(partial_proj, "expert", scatter_dimension=0, tiled=True)
    place = (moved_offs[None, :] == jnp.arange(tok_dev, dtype=jnp.int32)[:, None]).astype(bf16)
    placed = select_dot(place, projected)
    has_image = jnp.sum(place.astype(f32), axis=1, keepdims=True) > 0
    embed_own = jnp.where(has_image, placed, text_embed.astype(f32))
    normed_own = normalize(embed_own, norm_gain)
    normed = lax.all_gather(normed_own, "expert", axis=0, tiled=True)
    routes = lax.all_gather(
        jnp.concatenate([route_ids, route_wts], axis=1), "expert", axis=0, tiled=True
    )
    top_count = route_ids.shape[1]
    ids = routes[:, :top_count]
    weights = routes[:, top_count:]
    gate_s = jnp.dot(normed, shared_gate, preferred_element_type=f32)
    up_s = jnp.dot(normed, shared_up, preferred_element_type=f32)
    shared_hidden = (jax.nn.silu(gate_s) * up_s).astype(bf16)
    group_rows = normed.shape[0]
    n_pairs = group_rows * top_count
    capacity = 3 * group_rows * top_count // (2 * n_data)
    share = capacity // n_group
    flat_ids = ids.reshape(-1)
    onehot = (flat_ids[:, None] == jnp.arange(n_data, dtype=jnp.int32)[None, :]).astype(bf16)
    pair_iota = jnp.arange(n_pairs, dtype=jnp.int32)
    earlier = (pair_iota[None, :] < pair_iota[:, None]).astype(bf16)
    counts = select_dot(earlier, onehot)
    rank = jnp.sum(counts * onehot.astype(f32), axis=1).astype(jnp.int32)
    inside = rank // share == my_place
    row_of = jnp.where(inside, flat_ids * share + rank - my_place * share, -1)
    n_rows = n_data * share
    hit = (
        row_of.reshape(group_rows, top_count)[:, :, None]
        == jnp.arange(n_rows, dtype=jnp.int32)[None, None, :]
    )
    pick = jnp.sum(hit.astype(f32), axis=1).astype(bf16)
    send = select_dot(pick.T, normed).astype(bf16).reshape(n_data, share, width_model)
    arrived = lax.all_to_all(send, "dp", split_axis=0, concat_axis=0, tiled=True)
    slots = lax.all_gather(arrived.reshape(n_rows, width_model), "expert", axis=0, tiled=True)
    gate_e = jnp.dot(slots, expert_gate[0], preferred_element_type=f32)
    up_e = jnp.dot(slots, expert_up[0], preferred_element_type=f32)
    hidden_e = (jax.nn.silu(gate_e) * up_e).astype(bf16)
    partial_out = jnp.dot(hidden_e, expert_down[0], preferred_element_type=f32).astype(bf16)
    summed = lax.psum_scatter(partial_out, "expert", scatter_dimension=0, tiled=True)
    returned = lax.all_to_all(
        summed.reshape(n_data, share, width_model), "dp", split_axis=0, concat_axis=0, tiled=True
    ).reshape(n_rows, width_model)
    weights_f = weights.astype(f32)
    weights_n = weights_f / jnp.sum(weights_f, axis=1, keepdims=True)
    coef = jnp.sum(jnp.where(hit, weights_n[:, :, None], 0.0), axis=1)
    coef_hi = coef.astype(bf16)
    coef_lo = (coef - coef_hi.astype(f32)).astype(bf16)
    combined = select_dot(coef_hi, returned) + select_dot(coef_lo, returned)
    total = lax.psum_scatter(
        (jnp.dot(shared_hidden, shared_down, preferred_element_type=f32) + combined).astype(bf16),
        "expert",
        scatter_dimension=0,
        tiled=True,
    ).astype(f32)
    return (embed_own + total).astype(bf16)


def solution(mesh):
    return jax.shard_map(
        shards,
        mesh=mesh,
        in_specs=(
            P(("dp", "expert"), None),
            P(("dp", "expert"), None),
            P(("dp", "expert")),
            P(None, "expert"),
            P("expert", None),
            P(),
            P(None, "expert"),
            P(None, "expert"),
            P("expert", None),
            P("dp", None, "expert"),
            P("dp", None, "expert"),
            P("dp", "expert", None),
            P(("dp", "expert"), None),
            P(("dp", "expert"), None),
        ),
        out_specs=P(("dp", "expert"), None),
        check_vma=False,
    )
```

profile of v0, /device:TPU:2, one launch (start us, length us, event | category | flops | bytes accessed | tf_op | source)
XLA Modules:
  0.0 374.7 jit_solution(14832235509471755536)
XLA Ops:
  7.4 1.6 sort.17
  12.8 23.4 %all_to_all.15 = bf16[32,2,2368]{2,1,0:T(2,128)(2,1)S(1)} all-to-all(bf16[32,2,2368]{2,1,0:T(2,128)(2,1)S(1)} %reshape.103), channel_id=1, replica_groups=mesh['dp'=32,'expert'=8] {'dp'}, dimensions={0} | all-to-all | bytes 606208 | tf_op jit(solution)/shard_map/all_to_all | solution.py:47
  37.6 25.5 %all-gather.5.cloned.1.call-done = bf16[256,4608]{1,0:T(8,128)(2,1)} async-done(((bf16[32,4608]{1,0:T(8,128)(2,1)}), bf16[256,4608]{1,0:T(8,128)(2,1)}) %all-gather.5.cloned.1.call-update) | async-done | bytes 2359312 | tf_op jit(solution)/shard_map/all_gather | solution.py:51
  63.1 4.6 %convolution_convert_fusion.1 = bf16[256,2048]{1,0:T(8,128)(2,1)} fusion(bf16[256,2048]{1,0:T(8,128)(2,1)} %param.18, bf16[256,4608]{1,0:T(8,128)(2,1)} %all-gather.5.cloned.1.call-done, bf16[4608,256]{1,0:T(8,128)(2,1)S(1)} %copy-done), kind=kOutput, calls=%fused_computation.7 | convolution fusion | flops 873529344 | bytes 6815744 | tf_op jit(solution)/shard_map/dot_general | solution.py:55
  68.0 34.9 %reduce-scatter.4.cloned.1.call-done = bf16[32,2048]{1,0:T(8,128)(2,1)} async-done(((bf16[256,2048]{1,0:T(8,128)(2,1)}), bf16[32,2048]{1,0:T(8,128)(2,1)}) %reduce-scatter.4.cloned.1.call-update) | async-done | bytes 131088 | tf_op jit(solution)/shard_map/reduce_scatter | solution.py:56
  106.0 11.2 %all-gather = s32[8,64,4]{1,2,0:T(4,128)S(1)} all-gather(s32[1,64,4]{1,2,0:T(4,128)S(1)} %add_bitcast_fusion), channel_id=1, replica_groups=mesh['dp'=32,'expert'=8] {'expert'}, dimensions={0}, use_global_device_ids=true | all-gather | bytes 9216 | tf_op jit(solution)/shard_map/all_gather | solution.py:63
  119.5 13.4 %all-gather.7.cloned.1.call-done = bf16[512,2048]{1,0:T(8,128)(2,1)} async-done(((bf16[64,2048]{1,0:T(8,128)(2,1)}), bf16[512,2048]{1,0:T(8,128)(2,1)}) %all-gather.7.cloned.1.call-update) | async-done | bytes 2097168 | tf_op jit(solution)/shard_map/all_gather | solution.py:62
  132.9 2.3 convolution_convert_fusion.2
  136.5 36.9 %all_to_all.16 = bf16[32,6,2048]{2,1,0:T(8,128)(2,1)} all-to-all(bf16[32,6,2048]{2,1,0:T(8,128)(2,1)} %reshape.77), channel_id=1, replica_groups=mesh['dp'=32,'expert'=8] {'dp'}, dimensions={0} | all-to-all | bytes 1572864 | tf_op jit(solution)/shard_map/all_to_all | solution.py:91
  173.4 2.1 reshape.78
  175.8 40.9 %all-gather.9.cloned.1.call-done = bf16[1536,2048]{1,0:T(8,128)(2,1)} async-done(((bf16[192,2048]{1,0:T(8,128)(2,1)}), bf16[1536,2048]{1,0:T(8,128)(2,1)}) %all-gather.9.cloned.1.call-update) | async-done | bytes 6291472 | tf_op jit(solution)/shard_map/all_gather | solution.py:92
  216.7 6.0 %fusion.13 = f32[1536,176]{0,1:T(8,128)} fusion(bf16[1536,2048]{1,0:T(8,128)(2,1)} %all-gather.9.cloned.1.call-done, bf16[1,2048,176]{1,2,0:T(8,128)(2,1)S(1)} %copy-done.8), kind=kOutput, calls=%fused_computation.25 | convolution fusion | flops 1107296256 | bytes 8093696 | tf_op jit(solution)/shard_map/dot_general | solution.py:93
  222.7 10.0 %convolution_convert_fusion = bf16[1536,2048]{1,0:T(8,128)(2,1)} fusion(bf16[1536,2048]{1,0:T(8,128)(2,1)} %all-gather.9.cloned.1.call-done, f32[1536,176]{0,1:T(8,128)} %fusion.13, bf16[1,176,2048]{2,1,0:T(8,128)(2,1)} %param.25, bf16[1,2048,176]{1,2,0:T(8,128)(2,1)} %param.24), kind=kOutput, calls=%fused_computation.2 | convolution fusion | flops 2219360256 | bytes 15106048 | tf_op jit(solution)/shard_map/dot_general | solution.py:96
  232.8 45.3 %reduce-scatter.6.cloned.1.call-done = bf16[192,2048]{1,0:T(8,128)(2,1)} async-done(((bf16[1536,2048]{1,0:T(8,128)(2,1)}), bf16[192,2048]{1,0:T(8,128)(2,1)}) %reduce-scatter.6.cloned.1.call-update) | async-done | bytes 786448 | tf_op jit(solution)/shard_map/reduce_scatter | solution.py:97
  278.0 2.2 reshape.79
  280.2 10.2 %all-to-all-start.2 = ((bf16[32,6,2048]{2,1,0:T(8,128)(2,1)}), bf16[32,6,2048]{2,1,0:T(8,128)(2,1)}, u32[]{:S(2)}, u32[]{:S(2)}) async-start(bf16[32,6,2048]{2,1,0:T(8,128)(2,1)} %reshape.79), calls=%async_computation.4 | async-start | bytes 2097152 | tf_op jit(solution)/shard_map/all_to_all | solution.py:98
  290.5 3.8 %fusion.51 = f32[512,352]{0,1:T(8,128)} fusion(bf16[512,2048]{1,0:T(8,128)(2,1)} %all-gather.7.cloned.1.call-done, bf16[2048,352]{0,1:T(8,128)(2,1)} %param.20), kind=kOutput, calls=%fused_computation.91 | convolution fusion | flops 738197504 | bytes 4259840 | tf_op jit(solution)/shard_map/dot_general | solution.py:69
  294.3 22.0 %all-to-all-done.2 = bf16[32,6,2048]{2,1,0:T(8,128)(2,1)} async-done(((bf16[32,6,2048]{2,1,0:T(8,128)(2,1)}), bf16[32,6,2048]{2,1,0:T(8,128)(2,1)}, u32[]{:S(2)}, u32[]{:S(2)}) %all-to-all-start.2) | async-done | bytes 786464 | tf_op jit(solution)/shard_map/all_to_all | solution.py:98
  316.3 1.4 reshape.80
  317.7 2.7 fusion.25
  320.4 2.7 fusion.34
  323.1 8.7 %add_convert_fusion = bf16[512,2048]{1,0:T(8,128)(2,1)} fusion(f32[512,2048]{1,0:T(8,128)} %fusion.34, f32[512,2048]{1,0:T(8,128)} %fusion.25, bf16[352,2048]{1,0:T(8,128)(2,1)} %param.22, bf16[512,2048]{1,0:T(8,128)(2,1)} %all-gather.7.cloned.1.call-done, bf16[2048,352]{0,1:T(8,128)(2,1)} %param.21, f32[512,352]{0,1:T(8,128)} %fusion.51), kind=kOutput, calls=%fused_computation.3 | convolution fusion | flops 1480622080 | bytes 16187392 | tf_op jit(solution)/shard_map/dot_general | solution.py:108
  331.8 34.4 %reduce-scatter.8.cloned.1.call-done = bf16[64,2048]{1,0:T(8,128)(2,1)} async-done(((bf16[512,2048]{1,0:T(8,128)(2,1)}), bf16[64,2048]{1,0:T(8,128)(2,1)}) %reduce-scatter.8.cloned.1.call-update) | async-done | bytes 262160 | tf_op jit(solution)/shard_map/reduce_scatter | solution.py:107
  366.2 1.7 add_convert_fusion.1
  (66 shorter events, 13.1 us)
Async XLA Ops:
  6.5 56.6 %copy-start = (bf16[4608,256]{1,0:T(8,128)(2,1)S(1)}, bf16[4608,256]{1,0:T(8,128)(2,1)}, u32[]{:S(2)}) copy-start(bf16[4608,256]{1,0:T(8,128)(2,1)} %param.17) | copy-start | bytes 7077892
  6.5 3.8 %copy-start.1 = (bf16[32,4608]{1,0:T(8,128)(2,1)S(1)}, bf16[32,4608]{1,0:T(8,128)(2,1)}, u32[]{:S(2)}) copy-start(bf16[32,4608]{1,0:T(8,128)(2,1)} %param.15) | copy-start | bytes 884740
  6.5 56.6 %all-gather.5.cloned.1.call-start = ((), (), s32[]{:S(2)}) async-start(), calls=%async_computation.6 | async-start | bytes 2654208 | tf_op jit(solution)/shard_map/all_gather | solution.py:51
  37.5 65.4 %copy-start.4 = (bf16[64,2048]{1,0:T(8,128)(2,1)S(1)}, bf16[64,2048]{1,0:T(8,128)(2,1)}, u32[]{:S(2)}) copy-start(bf16[64,2048]{1,0:T(8,128)(2,1)} %param.14) | copy-start | bytes 786436
  37.5 67.5 %copy-start.5 = (f32[2048]{0:T(1024)S(1)}, f32[2048]{0:T(1024)}, u32[]{:S(2)}) copy-start(f32[2048]{0:T(1024)} %param.19) | copy-start | bytes 24580
  37.5 65.4 %reduce-scatter.4.cloned.1.call-start = ((), (), s32[]{:S(2)}) async-start(), calls=%async_computation.7 | async-start | bytes 1179648 | tf_op jit(solution)/shard_map/reduce_scatter | solution.py:56
  67.7 38.3 %copy-start.6 = (s32[64,2]{0,1:T(2,128)S(1)}, s32[64,2]{0,1:T(2,128)}, u32[]{:S(2)}) copy-start(s32[64,2]{0,1:T(2,128)} %param.27) | copy-start | bytes 1540
  67.7 38.3 %copy-start.7 = (s32[64,2]{0,1:T(2,128)S(1)}, s32[64,2]{0,1:T(2,128)}, u32[]{:S(2)}) copy-start(s32[64,2]{0,1:T(2,128)} %param.26) | copy-start | bytes 1540
  67.7 65.2 %all-gather.7.cloned.1.call-start = ((), (), s32[]{:S(2)}) async-start(), calls=%async_computation.8 | async-start | bytes 2359296 | tf_op jit(solution)/shard_map/all_gather | solution.py:62
  104.2 0.8 copy-start.2
  105.9 110.8 %all-gather.9.cloned.1.call-start = ((), (), s32[]{:S(2)}) async-start(), calls=%async_computation.9 | async-start | bytes 7077888 | tf_op jit(solution)/shard_map/all_gather | solution.py:92
  136.5 80.2 %copy-start.8 = (bf16[1,2048,176]{1,2,0:T(8,128)(2,1)S(1)}, bf16[1,2048,176]{1,2,0:T(8,128)(2,1)}, u32[]{:S(2)}) copy-start(bf16[1,2048,176]{1,2,0:T(8,128)(2,1)} %param.23) | copy-start | bytes 2162692
  175.6 102.5 %reduce-scatter.6.cloned.1.call-start = ((), (), s32[]{:S(2)}) async-start(), calls=%async_computation.10 | async-start | bytes 7077888 | tf_op jit(solution)/shard_map/reduce_scatter | solution.py:97
  280.2 36.1 %all-to-all-start.2 = ((bf16[32,6,2048]{2,1,0:T(8,128)(2,1)}), bf16[32,6,2048]{2,1,0:T(8,128)(2,1)}, u32[]{:S(2)}, u32[]{:S(2)}) async-start(bf16[32,6,2048]{2,1,0:T(8,128)(2,1)} %reshape.79), calls=%async_computation.4 | async-start | bytes 2097152 | tf_op jit(solution)/shard_map/all_to_all | solution.py:98
  290.4 75.7 %reduce-scatter.8.cloned.1.call-start = ((), (), s32[]{:S(2)}) async-start(), calls=%async_computation.11 | async-start | bytes 2359296 | tf_op jit(solution)/shard_map/reduce_scatter | solution.py:107
  331.8 34.4 %copy-start.3 = (f32[64,2048]{1,0:T(8,128)S(1)}, f32[64,2048]{1,0:T(8,128)}, u32[]{:S(2)}) copy-start(f32[64,2048]{1,0:T(8,128)} %copy-done.2) | copy-start | bytes 1572868
Sparse Core Ops, SparseCore 0:
  37.6 25.4 all-gather.4
  67.8 35.0 reduce-scatter.3
  106.0 26.8 all-gather.6
  175.7 40.9 all-gather.8
  232.9 45.0 reduce-scatter.5
  331.9 34.1 reduce-scatter.7
where the time goes:
time: 375 us
  waiting for transfers between devices  216 us (58%)
  blocking collectives  71.5 us (19%)
  matrix products  42.7 us (11%)
  between operations  13.7 us (4%)
  local copies, waits for them, and re-layouts  12.8 us (3%)
  starting transfers between devices  10.6 us (3%)
  other arithmetic  6.97 us (2%)
    reduce_scatter x1, waiting for transfers between devices, shards(): lax.psum_scatter(partial_out, 'expert', scatter_dimension=0, tiled=True)  45.3 us
    all_gather x1, waiting for transfers between devices, shards(): lax.all_gather(arrived.reshape(n_rows, width_model), 'expert', axis=0, ti...  40.9 us
    all_to_all x1, blocking collectives, shards(): lax.all_to_all(send, 'dp', split_axis=0, concat_axis=0, tiled=True)  36.9 us
    reduce_scatter x1, waiting for transfers between devices, shards(): lax.psum_scatter(partial_proj, 'expert', scatter_dimension=0, tiled=True)  34.9 us
    reduce_scatter x1, waiting for transfers between devices, shards(): lax.psum_scatter((jnp.dot(shared_hidden, shared_down, preferred_element_t...  34.4 us
    all_gather x1, waiting for transfers between devices, shards(): feats = lax.all_gather(moved_feats, 'expert', axis=0, tiled=True)  25.5 us
    all_to_all x1, blocking collectives, shards(): lax.all_to_all(packed, 'dp', split_axis=0, concat_axis=0, tiled=True)  23.4 us
    all_to_all x1, waiting for transfers between devices, shards(): lax.all_to_all(summed.reshape(n_data, share, width_model), 'dp', split_ax...  22 us
  transfers between devices with their start and end apart: 7, of which 7 were waited for; matrix products, arithmetic and copies ran while one was open for 2% of the time, Pallas kernels for 0%

commit v1 on v0

--- a/solution.py
+++ b/solution.py
@@ -2,6 +2,11 @@
 import jax.numpy as jnp
 from jax import lax
 from jax.sharding import PartitionSpec as P
+
+
+def gather_by_exchange(shard, axis, dim):
+    copies = jnp.concatenate([shard] * lax.axis_size(axis), axis=dim)
+    return lax.all_to_all(copies, axis, dim, dim, tiled=True)
 
 
 def normalize(rows, norm_gain):
@@ -89,7 +94,7 @@
     pick = jnp.sum(hit.astype(f32), axis=1).astype(bf16)
     send = select_dot(pick.T, normed).astype(bf16).reshape(n_data, share, width_model)
     arrived = lax.all_to_all(send, "dp", split_axis=0, concat_axis=0, tiled=True)
-    slots = lax.all_gather(arrived.reshape(n_rows, width_model), "expert", axis=0, tiled=True)
+    slots = gather_by_exchange(arrived.reshape(n_rows, width_model), "expert", 0)
     gate_e = jnp.dot(slots, expert_gate[0], preferred_element_type=f32)
     up_e = jnp.dot(slots, expert_up[0], preferred_element_type=f32)
     hidden_e = (jax.nn.silu(gate_e) * up_e).astype(bf16)

time: 375 us -> 409 us (1.091)
  blocking collectives: 71.5 us -> 147 us
  waiting for transfers between devices: 216 us -> 172 us
    all_to_all x0 -> x1, blocking collectives: none -> 76.1 us  [gather_by_exchange(): return lax.all_to_all(copies, axis, dim, dim, tiled=True)]
    all_gather x1 -> x0, waiting for transfers between devices: 40.9 us -> none  [shards(): lax.all_gather(arrived.reshape(n_rows, width_model), 'expert', axis=0, ti...]
  transfers between devices with their start and end apart: 7 -> 6, of which waited for: 7 -> 6; matrix products, arithmetic and copies ran while one was open for 2% -> 2% of each run, Pallas kernels for 0% -> 0%
where the time goes in v1:
time: 409 us; the launch traced here: 408 us
  waiting for transfers between devices  172 us (42%)
  blocking collectives  147 us (36%)
  matrix products  41.1 us (10%)
  local copies, waits for them, and re-layouts  16.4 us (4%)
  between operations  13.4 us (3%)
  starting transfers between devices  10.4 us (3%)
  other arithmetic  6.96 us (2%)
    all_to_all x1, blocking collectives, gather_by_exchange(): return lax.all_to_all(copies, axis, dim, dim, tiled=True)  76.1 us
    reduce_scatter x1, waiting for transfers between devices, shards(): lax.psum_scatter(partial_out, 'expert', scatter_dimension=0, tiled=True)  42.1 us
    all_to_all x1, blocking collectives, shards(): lax.all_to_all(send, 'dp', split_axis=0, concat_axis=0, tiled=True)  36.8 us
    reduce_scatter x1, waiting for transfers between devices, shards(): lax.psum_scatter(partial_proj, 'expert', scatter_dimension=0, tiled=True)  34.9 us
    reduce_scatter x1, waiting for transfers between devices, shards(): lax.psum_scatter((jnp.dot(shared_hidden, shared_down, preferred_element_t...  34.3 us
    all_gather x1, waiting for transfers between devices, shards(): feats = lax.all_gather(moved_feats, 'expert', axis=0, tiled=True)  25.5 us
    all_to_all x1, blocking collectives, shards(): lax.all_to_all(packed, 'dp', split_axis=0, concat_axis=0, tiled=True)  23.4 us
    all_to_all x1, waiting for transfers between devices, shards(): lax.all_to_all(summed.reshape(n_data, share, width_model), 'dp', split_ax...  22 us
  transfers between devices with their start and end apart: 6, of which 6 were waited for; matrix products, arithmetic and copies ran while one was open for 2% of the time, Pallas kernels for 0%

profile of v1, /device:TPU:2, one launch (start us, length us, event | category | flops | bytes accessed | tf_op | source)
XLA Modules:
  0.0 408.0 jit_solution(18132380290259138724)
XLA Ops:
  7.4 1.6 sort.17
  10.3 2.0 gather_fusion
  14.1 23.4 %all_to_all.27 = bf16[32,2,2368]{2,1,0:T(2,128)(2,1)S(1)} all-to-all(bf16[32,2,2368]{2,1,0:T(2,128)(2,1)S(1)} %reshape.105), channel_id=1, replica_groups=mesh['dp'=32,'expert'=8] {'dp'}, dimensions={0} | all-to-all | bytes 606208 | tf_op jit(solution)/shard_map/all_to_all | solution.py:52
  38.8 25.5 %all-gather.4.cloned.1.call-done = bf16[256,4608]{1,0:T(8,128)(2,1)} async-done(((bf16[32,4608]{1,0:T(8,128)(2,1)}), bf16[256,4608]{1,0:T(8,128)(2,1)}) %all-gather.4.cloned.1.call-update) | async-done | bytes 2359312 | tf_op jit(solution)/shard_map/all_gather | solution.py:56
  64.4 4.6 %convolution_convert_fusion.1 = bf16[256,2048]{1,0:T(8,128)(2,1)} fusion(bf16[256,2048]{1,0:T(8,128)(2,1)} %param.18, bf16[256,4608]{1,0:T(8,128)(2,1)} %all-gather.4.cloned.1.call-done, bf16[4608,256]{1,0:T(8,128)(2,1)S(1)} %copy-done), kind=kOutput, calls=%fused_computation.7 | convolution fusion | flops 873529344 | bytes 6815744 | tf_op jit(solution)/shard_map/dot_general | solution.py:60
  69.3 34.9 %reduce-scatter.4.cloned.1.call-done = bf16[32,2048]{1,0:T(8,128)(2,1)} async-done(((bf16[256,2048]{1,0:T(8,128)(2,1)}), bf16[32,2048]{1,0:T(8,128)(2,1)}) %reduce-scatter.4.cloned.1.call-update) | async-done | bytes 131088 | tf_op jit(solution)/shard_map/reduce_scatter | solution.py:61
  107.2 11.2 %all-gather = s32[8,64,4]{1,2,0:T(4,128)S(1)} all-gather(s32[1,64,4]{1,2,0:T(4,128)S(1)} %add_bitcast_fusion), channel_id=1, replica_groups=mesh['dp'=32,'expert'=8] {'expert'}, dimensions={0}, use_global_device_ids=true | all-gather | bytes 9216 | tf_op jit(solution)/shard_map/all_gather | solution.py:68
  120.8 13.4 %all-gather.6.cloned.1.call-done = bf16[512,2048]{1,0:T(8,128)(2,1)} async-done(((bf16[64,2048]{1,0:T(8,128)(2,1)}), bf16[512,2048]{1,0:T(8,128)(2,1)}) %all-gather.6.cloned.1.call-update) | async-done | bytes 2097168 | tf_op jit(solution)/shard_map/all_gather | solution.py:67
  134.2 2.3 convolution_convert_fusion.2
  137.7 36.8 %all_to_all.28 = bf16[32,6,2048]{2,1,0:T(8,128)(2,1)} all-to-all(bf16[32,6,2048]{2,1,0:T(8,128)(2,1)} %reshape.79), channel_id=1, replica_groups=mesh['dp'=32,'expert'=8] {'dp'}, dimensions={0} | all-to-all | bytes 1572864 | tf_op jit(solution)/shard_map/all_to_all | solution.py:96
  176.4 76.1 %all_to_all.29 = bf16[8,192,2048]{2,1,0:T(8,128)(2,1)S(1)} all-to-all(bf16[8,192,2048]{2,1,0:T(8,128)(2,1)S(1)} %bitcast.36), channel_id=1, replica_groups=mesh['dp'=32,'expert'=8] {'expert'}, dimensions={0} | all-to-all | bytes 12582912 | tf_op jit(solution)/shard_map/all_to_all | solution.py:9
  252.5 2.7 copy-done.1
  255.2 3.2 fusion.13
  258.4 11.2 %convolution_convert_fusion = bf16[1536,2048]{1,0:T(8,128)(2,1)} fusion(bf16[1536,2048]{1,0:T(8,128)(2,1)} %bitcast.38, f32[1536,176]{0,1:T(8,128)} %fusion.13, bf16[1,176,2048]{2,1,0:T(8,128)(2,1)S(1)} %copy-done.9, bf16[1,2048,176]{1,2,0:T(8,128)(2,1)} %param.24), kind=kOutput, calls=%fused_computation.2 | convolution fusion | flops 2219360256 | bytes 15106048 | tf_op jit(solution)/shard_map/dot_general | solution.py:101
  269.6 42.1 %reduce-scatter.6.cloned.1.call-done = bf16[192,2048]{1,0:T(8,128)(2,1)} async-done(((bf16[1536,2048]{1,0:T(8,128)(2,1)}), bf16[192,2048]{1,0:T(8,128)(2,1)}) %reduce-scatter.6.cloned.1.call-update) | async-done | bytes 786448 | tf_op jit(solution)/shard_map/reduce_scatter | solution.py:102
  311.7 2.2 reshape.81
  313.9 10.2 %all-to-all-start.3 = ((bf16[32,6,2048]{2,1,0:T(8,128)(2,1)}), bf16[32,6,2048]{2,1,0:T(8,128)(2,1)}, u32[]{:S(2)}, u32[]{:S(2)}) async-start(bf16[32,6,2048]{2,1,0:T(8,128)(2,1)} %reshape.81), calls=%async_computation.5 | async-start | bytes 2097152 | tf_op jit(solution)/shard_map/all_to_all | solution.py:103
  324.2 3.8 fusion.51
  328.0 22.0 %all-to-all-done.3 = bf16[32,6,2048]{2,1,0:T(8,128)(2,1)} async-done(((bf16[32,6,2048]{2,1,0:T(8,128)(2,1)}), bf16[32,6,2048]{2,1,0:T(8,128)(2,1)}, u32[]{:S(2)}, u32[]{:S(2)}) %all-to-all-start.3) | async-done | bytes 786464 | tf_op jit(solution)/shard_map/all_to_all | solution.py:103
  351.4 2.7 fusion.25
  354.1 2.7 fusion.34
  356.7 8.7 %add_convert_fusion = bf16[512,2048]{1,0:T(8,128)(2,1)} fusion(f32[512,2048]{1,0:T(8,128)} %fusion.34, f32[512,2048]{1,0:T(8,128)} %fusion.25, bf16[352,2048]{1,0:T(8,128)(2,1)} %param.22, bf16[512,2048]{1,0:T(8,128)(2,1)} %all-gather.6.cloned.1.call-done, bf16[2048,352]{0,1:T(8,128)(2,1)} %param.21, f32[512,352]{0,1:T(8,128)} %fusion.51), kind=kOutput, calls=%fused_computation.3 | convolution fusion | flops 1480622080 | bytes 16187392 | tf_op jit(solution)/shard_map/dot_general | solution.py:113
  365.5 34.3 %reduce-scatter.8.cloned.1.call-done = bf16[64,2048]{1,0:T(8,128)(2,1)} async-done(((bf16[512,2048]{1,0:T(8,128)(2,1)}), bf16[64,2048]{1,0:T(8,128)(2,1)}) %reduce-scatter.8.cloned.1.call-update) | async-done | bytes 262160 | tf_op jit(solution)/shard_map/reduce_scatter | solution.py:112
  399.8 1.7 add_convert_fusion.1
  (74 shorter events, 15.3 us)
Async XLA Ops:
  6.5 57.9 %copy-start = (bf16[4608,256]{1,0:T(8,128)(2,1)S(1)}, bf16[4608,256]{1,0:T(8,128)(2,1)}, u32[]{:S(2)}) copy-start(bf16[4608,256]{1,0:T(8,128)(2,1)} %param.17) | copy-start | bytes 7077892
  6.5 57.8 %all-gather.4.cloned.1.call-start = ((), (), s32[]{:S(2)}) async-start(), calls=%async_computation.7 | async-start | bytes 2654208 | tf_op jit(solution)/shard_map/all_gather | solution.py:56
  38.8 65.4 %copy-start.4 = (bf16[64,2048]{1,0:T(8,128)(2,1)S(1)}, bf16[64,2048]{1,0:T(8,128)(2,1)}, u32[]{:S(2)}) copy-start(bf16[64,2048]{1,0:T(8,128)(2,1)} %param.14) | copy-start | bytes 786436
  38.8 67.5 %copy-start.5 = (f32[2048]{0:T(1024)S(1)}, f32[2048]{0:T(1024)}, u32[]{:S(2)}) copy-start(f32[2048]{0:T(1024)} %param.19) | copy-start | bytes 24580
  38.8 65.4 %reduce-scatter.4.cloned.1.call-start = ((), (), s32[]{:S(2)}) async-start(), calls=%async_computation.8 | async-start | bytes 1179648 | tf_op jit(solution)/shard_map/reduce_scatter | solution.py:61
  69.0 38.3 %copy-start.6 = (s32[64,2]{0,1:T(2,128)S(1)}, s32[64,2]{0,1:T(2,128)}, u32[]{:S(2)}) copy-start(s32[64,2]{0,1:T(2,128)} %param.27) | copy-start | bytes 1540
  69.0 38.3 %copy-start.7 = (s32[64,2]{0,1:T(2,128)S(1)}, s32[64,2]{0,1:T(2,128)}, u32[]{:S(2)}) copy-start(s32[64,2]{0,1:T(2,128)} %param.26) | copy-start | bytes 1540
  69.0 65.2 %all-gather.6.cloned.1.call-start = ((), (), s32[]{:S(2)}) async-start(), calls=%async_computation.9 | async-start | bytes 2359296 | tf_op jit(solution)/shard_map/all_gather | solution.py:67
  105.5 0.8 copy-start.2
  107.2 204.5 %reduce-scatter.6.cloned.1.call-start = ((), (), s32[]{:S(2)}) async-start(), calls=%async_computation.10 | async-start | bytes 7077888 | tf_op jit(solution)/shard_map/reduce_scatter | solution.py:102
  176.4 78.8 %copy-start.8 = (bf16[1,2048,176]{1,2,0:T(8,128)(2,1)S(1)}, bf16[1,2048,176]{1,2,0:T(8,128)(2,1)}, u32[]{:S(2)}) copy-start(bf16[1,2048,176]{1,2,0:T(8,128)(2,1)} %param.23) | copy-start | bytes 2162692
  252.5 2.7 copy-start.1
  255.1 3.2 copy-start.9
  313.9 36.1 %all-to-all-start.3 = ((bf16[32,6,2048]{2,1,0:T(8,128)(2,1)}), bf16[32,6,2048]{2,1,0:T(8,128)(2,1)}, u32[]{:S(2)}, u32[]{:S(2)}) async-start(bf16[32,6,2048]{2,1,0:T(8,128)(2,1)} %reshape.81), calls=%async_computation.5 | async-start | bytes 2097152 | tf_op jit(solution)/shard_map/all_to_all | solution.py:103
  324.1 75.7 %reduce-scatter.8.cloned.1.call-start = ((), (), s32[]{:S(2)}) async-start(), calls=%async_computation.11 | async-start | bytes 2359296 | tf_op jit(solution)/shard_map/reduce_scatter | solution.py:112
  365.4 34.3 %copy-start.3 = (f32[64,2048]{1,0:T(8,128)S(1)}, f32[64,2048]{1,0:T(8,128)}, u32[]{:S(2)}) copy-start(f32[64,2048]{1,0:T(8,128)} %copy-done.2) | copy-start | bytes 1572868
Sparse Core Ops, SparseCore 0:
  38.9 25.4 all-gather.3
  69.1 35.0 reduce-scatter.3
  107.3 26.8 all-gather.5
  269.8 41.9 reduce-scatter.5
  365.6 34.1 reduce-scatter.7
